TPU v7x, 32 devices: a whole 2x2x4 slice. The times are simulated.
32 devices in a mesh: exp: 8 (over z, x), rep: 4 (over y, core).
Axes of the slice: x: 2, y: 2, z: 4, core: 2. Of those that a mesh axis runs over, the one named last changes fastest.
Arguments:
- tokens: bfloat16 [18432, 768], P(('exp', 'rep')), may hold values from -6 to 6
- ln1_gain: bfloat16 [768], P(('exp', 'rep')), may hold values from 0.3984375 to 1.59375
- ln1_bias: bfloat16 [768], P(('exp', 'rep')), may hold values from -1.1953125 to 1.1953125
- w_qkv: bfloat16 [768, 2304], P(('exp', 'rep')), may hold values from -0.21875 to 0.21875
- w_out: bfloat16 [768, 768], P(('exp', 'rep')), may hold values from -2.5 to 2.5
- ln2_gain: bfloat16 [768], P(('exp', 'rep')), may hold values from 0.3984375 to 1.59375
- ln2_bias: bfloat16 [768], P(('exp', 'rep')), may hold values from -0.59765625 to 0.59765625
- w_router: bfloat16 [768, 8], P(('exp', 'rep')), may hold values from -0.109375 to 0.109375
- w_in: bfloat16 [8, 768, 3072], P('exp'), may hold values from -0.21875 to 0.21875
- b_in: bfloat16 [8, 3072], P('exp'), may hold values from -1.796875 to 1.796875
- w_back: bfloat16 [8, 3072, 768], P('exp'), may hold values from -0.625 to 0.625
- b_back: bfloat16 [8, 768], P('exp'), may hold values from -2.390625 to 2.390625
- lengths: int32 [32, 3], P(('exp', 'rep')), may hold values from 1 to 400, 576 in all within a row
- routes: int32 [18432, 2], P(('exp', 'rep')), may hold values from 0 to 7, all different within a row
- priority: int32 [18432], P(('exp', 'rep')), may hold values from 0 to 575, as said below
- padding: int32 [18432], P(('exp', 'rep')), may hold values 0 or 1
- cotangent: bfloat16 [18432, 768], P(('exp', 'rep')), may hold values from -6 to 6
Outputs:
- output: bfloat16 [18432, 768], P(('exp', 'rep'))
- grad_tokens: float32 [18432, 768], P(('exp', 'rep'))
- grad_ln1_gain: float32 [768], P(('exp', 'rep'))
- grad_ln1_bias: float32 [768], P(('exp', 'rep'))
- grad_w_qkv: float32 [768, 2304], P(('exp', 'rep'))
- grad_w_out: float32 [768, 768], P(('exp', 'rep'))
- grad_ln2_gain: float32 [768], P(('exp', 'rep'))
- grad_ln2_bias: float32 [768], P(('exp', 'rep'))
- grad_w_router: float32 [768, 8], P(('exp', 'rep'))
- grad_w_in: float32 [8, 768, 3072], P('exp')
- grad_b_in: float32 [8, 3072], P('exp')
- grad_w_back: float32 [8, 3072, 768], P('exp')
- grad_b_back: float32 [8, 768], P('exp')
Inputs may be any that keep to these rules, and one draw needn't show every extreme that they name: `routes`: each row names two different experts. `priority`: in each aligned group of 576 patches every value 0 to 575 appears once. `lengths`: each row sums to 576; its largest entry is 400.
All inputs are finite; a program needn't handle non-finite values. No bound on the sum of `padding` on one device may be relied on, other than what follows from the above.
Results may differ from a plain program's by a relative error of at most 0.014.
Values may be sent and summed in bfloat16 or wider, within the bound.
A program may use at most 192 MiB of HBM per device.

v0:
```python
import jax
import jax.numpy as jnp
from jax import lax
from jax.sharding import PartitionSpec as P

D = 768
HEADS = 12
HEAD = 64
SLOTS = 576
ROWS_DEV = 1
TOK_DEV = 576
root_half = 0.7071067811865476
inverse_root_tau = 0.3989422804014327
contract_first = (((0,), (0,)), ((), ()))
contract_last = (((1,), (1,)), ((), ()))


def norm_forward(inputs, gain, offset):
    center = inputs - jnp.mean(inputs, axis=-1, keepdims=True)
    inverse = lax.rsqrt(jnp.mean(center * center, axis=-1, keepdims=True) + 1e-06)
    normal = center * inverse
    return (normal * gain.astype(jnp.float32) + offset.astype(jnp.float32), normal, inverse)


def norm_backward(grad, normal, inverse, gain):
    scaled = grad * gain.astype(jnp.float32)
    grad_in = inverse * (
        scaled
        - jnp.mean(scaled, axis=-1, keepdims=True)
        - normal * jnp.mean(scaled * normal, axis=-1, keepdims=True)
    )
    return (grad_in, jnp.sum(grad * normal, axis=0), jnp.sum(grad, axis=0))


def gelu_slope(pre):
    return 0.5 * (1.0 + lax.erf(pre * root_half)) + pre * inverse_root_tau * jnp.exp(
        -0.5 * pre * pre
    )


def row_masks(lengths, padding):
    bounds = jnp.cumsum(lengths, axis=1)
    places = jnp.arange(SLOTS, dtype=jnp.int32)
    segments = jnp.sum((places[None, :, None] >= bounds[:, None, :]).astype(jnp.int32), axis=2)
    live = padding.reshape(ROWS_DEV, SLOTS) == 1
    same = segments[:, :, None] == segments[:, None, :]
    diagonal = places[:, None] == places[None, :]
    return same & (live[:, None, :] | diagonal[None])


def split_heads(qkv_row):
    query = qkv_row[:, :D].reshape(SLOTS, HEADS, HEAD)
    keys = qkv_row[:, D : 2 * D].reshape(SLOTS, HEADS, HEAD)
    values = qkv_row[:, 2 * D :].reshape(SLOTS, HEADS, HEAD)
    return (query, keys, values)


def masked_scores(query, keys, allowed_row):
    scores = jnp.einsum("qhc,khc->hqk", query, keys, preferred_element_type=jnp.float32) * HEAD ** (
        -0.5
    )
    return jnp.where(allowed_row[None], scores, -1e30)


def attend_forward(qkv_row, allowed_row):
    query, keys, values = split_heads(qkv_row)
    scores = masked_scores(query, keys, allowed_row)
    top = jnp.max(scores, axis=-1, keepdims=True)
    expo = jnp.exp(scores - top)
    total = jnp.sum(expo, axis=-1, keepdims=True)
    probs = (expo / total).astype(jnp.bfloat16)
    mixed = jnp.einsum("hqk,khc->qhc", probs, values, preferred_element_type=jnp.float32)
    return (mixed.reshape(SLOTS, D), top + jnp.log(total))


def attend_backward(qkv_row, allowed_row, lse_row, grad_row):
    query, keys, values = split_heads(qkv_row)
    probs = jnp.exp(masked_scores(query, keys, allowed_row) - lse_row)
    grad_mixed = grad_row.reshape(SLOTS, HEADS, HEAD)
    grad_probs = jnp.einsum("qhc,khc->hqk", grad_mixed, values, preferred_element_type=jnp.float32)
    grad_values = jnp.einsum(
        "hqk,qhc->khc", probs.astype(jnp.bfloat16), grad_mixed, preferred_element_type=jnp.float32
    )
    grad_scores = (
        probs * (grad_probs - jnp.sum(probs * grad_probs, axis=-1, keepdims=True))
    ).astype(jnp.bfloat16)
    grad_query = jnp.einsum(
        "hqk,khc->qhc", grad_scores, keys, preferred_element_type=jnp.float32
    ) * HEAD ** (-0.5)
    grad_keys = jnp.einsum(
        "hqk,qhc->khc", grad_scores, query, preferred_element_type=jnp.float32
    ) * HEAD ** (-0.5)
    joined = jnp.concatenate(
        [grad_query.reshape(SLOTS, D), grad_keys.reshape(SLOTS, D), grad_values.reshape(SLOTS, D)],
        axis=1,
    )
    return joined.astype(jnp.bfloat16)


def dispatch_tables(routes, priority, padding, experts, capacity):
    labels = jnp.arange(experts, dtype=jnp.int32)
    first_hot = (routes[:, 0:1] == labels[None, :]).astype(jnp.bfloat16)
    second_hot = (routes[:, 1:2] == labels[None, :]).astype(jnp.bfloat16)
    live = padding[:, None].astype(jnp.bfloat16)
    earlier = (priority[None, :] < priority[:, None]).astype(jnp.bfloat16)
    before_first = jnp.dot(earlier, first_hot * live, preferred_element_type=jnp.float32)
    first_counts = jnp.sum((first_hot * live).astype(jnp.float32), axis=0)
    before_second = (
        jnp.dot(earlier, second_hot * live, preferred_element_type=jnp.float32)
        + first_counts[None, :]
    )
    place_first = jnp.sum(before_first * first_hot, axis=1).astype(jnp.int32)
    place_second = jnp.sum(before_second * second_hot, axis=1).astype(jnp.int32)
    kept_first = (padding == 1) & (place_first < capacity)
    kept_second = (padding == 1) & (place_second < capacity)
    slot_labels = jnp.arange(experts * capacity, dtype=jnp.int32)
    slot_first = routes[:, 0] * capacity + place_first
    slot_second = routes[:, 1] * capacity + place_second
    pick_first = ((slot_first[:, None] == slot_labels[None, :]) & kept_first[:, None]).astype(
        jnp.bfloat16
    )
    pick_second = ((slot_second[:, None] == slot_labels[None, :]) & kept_second[:, None]).astype(
        jnp.bfloat16
    )
    return (first_hot.astype(jnp.float32), second_hot.astype(jnp.float32), pick_first, pick_second)


def on_device(
    tokens,
    ln1_gain,
    ln1_bias,
    w_qkv,
    w_out,
    ln2_gain,
    ln2_bias,
    w_router,
    w_in,
    b_in,
    w_back,
    b_back,
    lengths,
    routes,
    priority,
    padding,
    cotangent,
):
    experts = lax.axis_size("exp")
    capacity = (TOK_DEV * 210 + experts * 100 - 1) // (experts * 100)
    dense = (
        lax.all_gather(ln1_gain, ("exp", "rep"), axis=0, tiled=True),
        lax.all_gather(ln1_bias, ("exp", "rep"), axis=0, tiled=True),
        lax.all_gather(w_qkv, ("exp", "rep"), axis=0, tiled=True),
        lax.all_gather(w_out, ("exp", "rep"), axis=0, tiled=True),
        lax.all_gather(ln2_gain, ("exp", "rep"), axis=0, tiled=True),
        lax.all_gather(ln2_bias, ("exp", "rep"), axis=0, tiled=True),
        lax.all_gather(w_router, ("exp", "rep"), axis=0, tiled=True),
    )
    gain_one, bias_one, qkv_weight, out_weight, gain_two, bias_two, router_weight = dense
    inputs = tokens.astype(jnp.float32)
    normed, normal_one, inverse_one = norm_forward(inputs, gain_one, bias_one)
    normed_low = normed.astype(jnp.bfloat16)
    qkv = (
        jnp.dot(normed_low, qkv_weight, preferred_element_type=jnp.float32)
        .astype(jnp.bfloat16)
        .reshape(ROWS_DEV, SLOTS, 3 * D)
    )
    allowed = row_masks(lengths, padding)
    mixed, lse = lax.map(lambda pair: attend_forward(pair[0], pair[1]), (qkv, allowed))
    mixed_low = mixed.reshape(TOK_DEV, D).astype(jnp.bfloat16)
    resid = inputs + jnp.dot(mixed_low, out_weight, preferred_element_type=jnp.float32)
    routed_float, normal_two, inverse_two = norm_forward(resid, gain_two, bias_two)
    routed = routed_float.astype(jnp.bfloat16)
    logits = jnp.dot(routed, router_weight, preferred_element_type=jnp.float32)
    probs = jax.nn.softmax(logits, axis=-1)
    first_hot, second_hot, pick_first, pick_second = dispatch_tables(
        routes, priority, padding, experts, capacity
    )
    picks = pick_first + pick_second
    buffer = lax.dot_general(picks, routed, contract_first, preferred_element_type=jnp.float32)
    buffer = buffer.astype(jnp.bfloat16).reshape(experts, capacity, D)
    received_part = lax.all_to_all(buffer, "exp", split_axis=0, concat_axis=0, tiled=True)
    pre_part = jnp.einsum(
        "scd,df->scf", received_part, w_in[0], preferred_element_type=jnp.float32
    ) + b_in[0].astype(jnp.float32)
    active_part = jax.nn.gelu(pre_part, approximate=False).astype(jnp.bfloat16)
    result_part = jnp.einsum(
        "scf,fd->scd", active_part, w_back[0], preferred_element_type=jnp.float32
    ) + b_back[0].astype(jnp.float32)
    returned = lax.all_to_all(
        result_part.astype(jnp.bfloat16), "exp", split_axis=0, concat_axis=0, tiled=True
    )
    returned_flat = returned.reshape(experts * capacity, D)
    picked_first = jnp.dot(pick_first, returned_flat, preferred_element_type=jnp.float32)
    picked_second = jnp.dot(pick_second, returned_flat, preferred_element_type=jnp.float32)
    gate_first = jnp.sum(probs * first_hot, axis=1)
    gate_second = jnp.sum(probs * second_hot, axis=1)
    output = resid + gate_first[:, None] * picked_first + gate_second[:, None] * picked_second
    grad_out = cotangent.astype(jnp.float32)
    gated_first = (gate_first[:, None] * grad_out).astype(jnp.bfloat16)
    gated_second = (gate_second[:, None] * grad_out).astype(jnp.bfloat16)
    grad_slots = lax.dot_general(
        pick_first, gated_first, contract_first, preferred_element_type=jnp.float32
    )
    grad_slots = grad_slots + lax.dot_general(
        pick_second, gated_second, contract_first, preferred_element_type=jnp.float32
    )
    grad_results = lax.all_to_all(
        grad_slots.astype(jnp.bfloat16).reshape(experts, capacity, D),
        "exp",
        split_axis=0,
        concat_axis=0,
        tiled=True,
    )
    pre = jnp.einsum(
        "scd,df->scf", received_part, w_in[0], preferred_element_type=jnp.float32
    ) + b_in[0].astype(jnp.float32)
    active = jax.nn.gelu(pre, approximate=False).astype(jnp.bfloat16)
    grad_w_back = jnp.einsum(
        "scf,scd->fd", active, grad_results, preferred_element_type=jnp.float32
    )
    grad_b_back = jnp.sum(grad_results.astype(jnp.float32), axis=(0, 1))
    grad_active = jnp.einsum(
        "scd,fd->scf", grad_results, w_back[0], preferred_element_type=jnp.float32
    )
    grad_pre = (grad_active * gelu_slope(pre)).astype(jnp.bfloat16)
    grad_w_in = jnp.einsum(
        "scd,scf->df", received_part, grad_pre, preferred_element_type=jnp.float32
    )
    grad_b_in = jnp.sum(grad_pre.astype(jnp.float32), axis=(0, 1))
    expert_sums = (
        lax.psum(grad_w_in.astype(jnp.bfloat16), "rep").astype(jnp.float32),
        lax.psum(grad_b_in.astype(jnp.bfloat16), "rep").astype(jnp.float32),
        lax.psum(grad_w_back.astype(jnp.bfloat16), "rep").astype(jnp.float32),
        lax.psum(grad_b_back.astype(jnp.bfloat16), "rep").astype(jnp.float32),
    )
    grad_received = jnp.einsum(
        "scf,df->scd", grad_pre, w_in[0], preferred_element_type=jnp.float32
    ).astype(jnp.bfloat16)
    grad_buffer = lax.all_to_all(
        grad_received, "exp", split_axis=0, concat_axis=0, tiled=True
    ).reshape(experts * capacity, D)
    grad_gate_first = jnp.sum(grad_out * picked_first, axis=1)
    grad_gate_second = jnp.sum(grad_out * picked_second, axis=1)
    grad_probs = grad_gate_first[:, None] * first_hot + grad_gate_second[:, None] * second_hot
    grad_logits = (
        probs * (grad_probs - jnp.sum(probs * grad_probs, axis=1, keepdims=True))
    ).astype(jnp.bfloat16)
    dense_back = (
        lax.all_gather(ln1_gain, ("exp", "rep"), axis=0, tiled=True),
        lax.all_gather(ln1_bias, ("exp", "rep"), axis=0, tiled=True),
        lax.all_gather(w_qkv, ("exp", "rep"), axis=0, tiled=True),
        lax.all_gather(w_out, ("exp", "rep"), axis=0, tiled=True),
        lax.all_gather(ln2_gain, ("exp", "rep"), axis=0, tiled=True),
        lax.all_gather(ln2_bias, ("exp", "rep"), axis=0, tiled=True),
        lax.all_gather(w_router, ("exp", "rep"), axis=0, tiled=True),
    )
    gain_one, bias_one, qkv_weight, out_weight, gain_two, bias_two, router_weight = dense_back
    grad_router = lax.dot_general(
        routed, grad_logits, contract_first, preferred_element_type=jnp.float32
    )
    grad_routed = jnp.dot(picks, grad_buffer, preferred_element_type=jnp.float32)
    grad_routed = grad_routed + lax.dot_general(
        grad_logits, router_weight, contract_last, preferred_element_type=jnp.float32
    )
    grad_norm_two, grad_gain_two, grad_bias_two = norm_backward(
        grad_routed, normal_two, inverse_two, gain_two
    )
    grad_resid = grad_out + grad_norm_two
    grad_attn = grad_resid.astype(jnp.bfloat16)
    grad_out_weight = lax.dot_general(
        mixed_low, grad_attn, contract_first, preferred_element_type=jnp.float32
    )
    grad_mixed = lax.dot_general(
        grad_attn, out_weight, contract_last, preferred_element_type=jnp.float32
    )
    grad_mixed = grad_mixed.astype(jnp.bfloat16).reshape(ROWS_DEV, SLOTS, D)
    grad_qkv = lax.map(
        lambda group: attend_backward(group[0], group[1], group[2], group[3]),
        (qkv, allowed, lse, grad_mixed),
    )
    grad_qkv = grad_qkv.reshape(TOK_DEV, 3 * D)
    grad_qkv_weight = lax.dot_general(
        normed_low, grad_qkv, contract_first, preferred_element_type=jnp.float32
    )
    grad_normed = lax.dot_general(
        grad_qkv, qkv_weight, contract_last, preferred_element_type=jnp.float32
    )
    grad_norm_one, grad_gain_one, grad_bias_one = norm_backward(
        grad_normed, normal_one, inverse_one, gain_one
    )
    grad_tokens = grad_resid + grad_norm_one
    dense_grads = (
        lax.psum_scatter(grad_gain_one, ("exp", "rep"), scatter_dimension=0, tiled=True),
        lax.psum_scatter(grad_bias_one, ("exp", "rep"), scatter_dimension=0, tiled=True),
        lax.psum_scatter(grad_qkv_weight, ("exp", "rep"), scatter_dimension=0, tiled=True),
        lax.psum_scatter(grad_out_weight, ("exp", "rep"), scatter_dimension=0, tiled=True),
        lax.psum_scatter(grad_gain_two, ("exp", "rep"), scatter_dimension=0, tiled=True),
        lax.psum_scatter(grad_bias_two, ("exp", "rep"), scatter_dimension=0, tiled=True),
        lax.psum_scatter(grad_router, ("exp", "rep"), scatter_dimension=0, tiled=True),
    )
    return (
        output.astype(jnp.bfloat16),
        grad_tokens,
        dense_grads[0],
        dense_grads[1],
        dense_grads[2],
        dense_grads[3],
        dense_grads[4],
        dense_grads[5],
        dense_grads[6],
        expert_sums[0][None],
        expert_sums[1][None],
        expert_sums[2][None],
        expert_sums[3][None],
    )


def solution(mesh):
    return jax.shard_map(
        on_device,
        mesh=mesh,
        in_specs=(
            P(("exp", "rep"), None),
            P(("exp", "rep")),
            P(("exp", "rep")),
            P(("exp", "rep"), None),
            P(("exp", "rep"), None),
            P(("exp", "rep")),
            P(("exp", "rep")),
            P(("exp", "rep"), None),
            P("exp", None, None),
            P("exp", None),
            P("exp", None, None),
            P("exp", None),
            P(("exp", "rep"), None),
            P(("exp", "rep"), None),
            P(("exp", "rep")),
            P(("exp", "rep")),
            P(("exp", "rep"), None),
        ),
        out_specs=(
            P(("exp", "rep"), None),
            P(("exp", "rep"), None),
            P(("exp", "rep")),
            P(("exp", "rep")),
            P(("exp", "rep"), None),
            P(("exp", "rep"), None),
            P(("exp", "rep")),
            P(("exp", "rep")),
            P(("exp", "rep"), None),
            P("exp", None, None),
            P("exp", None),
            P("exp", None, None),
            P("exp", None),
        ),
        check_vma=False,
    )
```

profile of v0, /device:TPU:0, one launch (start us, length us, event | category | flops | bytes accessed | tf_op | source)
XLA Modules:
  0.0 835.7 jit_solution(4616695605341948638)
XLA Ops:
  15.5 42.2 %all-reduce.10 = (bf16[768]{0:T(1024)(128)(2,1)S(1)}, bf16[768]{0:T(1024)(128)(2,1)S(1)}, bf16[768]{0:T(1024)(128)(2,1)S(1)}, bf16[768]{0:T(1024)(128)(2,1)S(1)}) all-reduce(bf16[768]{0:T(1024)(128)(2,1)S(1)} %dynamic-update-slice.1, bf16[768]{0:T(1024)(128)(2,1)S(1)} %dynamic-update-slice, ...), channel_id=1, replica_groups=mesh['exp'=8,'rep'=4] {'exp','rep'}, use_global_device_ids=true, to_apply=%add.1 | all-reduce | flops 3072 | bytes 12288
  64.7 9.0 %all-gather.4.cloned.1.call-done = bf16[768,2304]{1,0:T(8,128)(2,1)} async-done(((bf16[24,2304]{1,0:T(8,128)(2,1)}), bf16[768,2304]{1,0:T(8,128)(2,1)}) %all-gather.4.cloned.1.call-update) | async-done | bytes 3538960 | tf_op jit(solution)/shard_map/all_gather | solution.py:152
  73.7 4.7 convolution_convert_fusion
  80.1 1.9 copy.61
  83.4 8.0 fusion.141
  91.4 8.6 %fusion = f32[12,576]{1,0:T(8,128)S(1)} fusion(f32[12,576,576]{1,2,0:T(8,128)} %get-tuple-element.84, f32[12,576]{1,0:T(8,128)S(1)} %get-tuple-element.83), kind=kLoop, calls=%fused_computation.8 | loop fusion | flops 7955712 | bytes 15980544 | tf_op jit(solution)/shard_map/while/body/eval_jaxpr/reduce_sum | solution.py:70
  100.0 10.3 %fusion.81 = bf16[12,64,576]{2,1,0:T(8,128)(2,1)} fusion(bf16[576,12,64]{0,2,1:T(8,128)(2,1)S(1)} %bitcast.102, f32[12,576,576]{1,2,0:T(8,128)} %get-tuple-element.84, f32[12,576]{1,0:T(8,128)S(1)} %fusion, f32[12,576]{1,0:T(8,128)S(1)} %get-tuple-element.83), kind=kOutput, calls=%fused_computation.121 | convolution fusion | flops 521994240 | bytes 17750016 | tf_op jit(solution)/shard_map/while/body/eval_jaxpr/hqk,khc->qhc/dot_general | solution.py:72
  110.3 19.1 %all-gather.6.cloned.1.call-done = bf16[768,768]{1,0:T(8,128)(2,1)} async-done(((bf16[24,768]{1,0:T(8,128)(2,1)}), bf16[768,768]{1,0:T(8,128)(2,1)}) %all-gather.6.cloned.1.call-update) | async-done | bytes 1179664 | tf_op jit(solution)/shard_map/all_gather | solution.py:153
  129.4 2.6 fusion.142
  132.7 3.5 convolution_convert_fusion.1
  136.2 5.1 all-to-all-start
  141.4 43.8 %all-to-all-done = bf16[8,152,768]{2,1,0:T(8,128)(2,1)} async-done(((bf16[8,152,768]{2,1,0:T(8,128)(2,1)}), bf16[8,152,768]{2,1,0:T(8,128)(2,1)}, u32[]{:S(2)}, u32[]{:S(2)}) %all-to-all-start) | async-done | bytes 1867808 | tf_op jit(solution)/shard_map/all_to_all | solution.py:181
  185.1 12.7 %fusion.30 = (u8[152,3072]{1,0:T(8,128)(4,1)S(1)}, u8[152,3072]{1,0:T(8,128)(4,1)S(1)}, f32[8,152,3072]{2,1,0:T(8,128)S(1)}) fusion(f32[3072]{0:T(1024)S(1)} %bitcast.113, bf16[8,152,768]{2,1,0:T(8,128)(2,1)} %all-to-all-done, bf16[1,768,3072]{2,1,0:T(8,128)(2,1)} %param.25), kind=kOutput, calls=%fused_computation.54 | convolution fusion | flops 5789171712 | bytes 22474752 | tf_op jit(solution)/shard_map/scd,df->scf/dot_general | solution.py:182
  197.9 34.1 %fusion.3 = bf16[8,152,3072]{2,1,0:T(8,128)(2,1)S(1)} fusion(f32[8,152,3072]{2,1,0:T(8,128)S(1)} %get-tuple-element.87, f32[3072]{0:T(1024)S(1)} %bitcast.114, u8[152,3072]{1,0:T(8,128)(4,1)S(1)} %get-tuple-element.47, u8[152,3072]{1,0:T(8,128)(4,1)S(1)} %get-tuple-element.46), kind=kLoop, calls=%fused_computation.11 | loop fusion | flops 265224192 | bytes 23359488 | tf_op jit(solution)/shard_map/convert_element_type | solution.py:185
  232.0 3.1 copy-done.10
  235.1 9.4 %add_convert_fusion = bf16[8,152,768]{2,1,0:T(8,128)(2,1)} fusion(f32[768]{0:T(1024)S(1)} %convert_reduce_fusion.2, bf16[8,152,3072]{2,1,0:T(8,128)(2,1)S(1)} %fusion.3, bf16[1,3072,768]{2,1,0:T(8,128)(2,1)} %param.27), kind=kOutput, calls=%fused_computation.52 | convolution fusion | flops 5739675648 | bytes 14060544 | tf_op jit(solution)/shard_map/scf,fd->scd/dot_general | solution.py:186
  244.5 4.4 all-to-all-start.1
  249.0 65.3 %all-gather = bf16[32,24,8]{1,2,0:T(8,128)(2,1)S(1)} all-gather(bf16[1,24,8]{1,2,0:T(8,128)(2,1)S(1)} %bitcast.116), channel_id=1, replica_groups=mesh['exp'=8,'rep'=4] {'exp','rep'}, dimensions={0}, use_global_device_ids=true | all-gather | bytes 12672 | tf_op jit(solution)/shard_map/all_gather | solution.py:156
  314.9 3.1 fusion.40
  318.0 5.0 fusion.68
  323.1 2.1 fusion.33
  325.2 2.2 fusion.31
  327.5 50.3 %all_to_all.20 = bf16[8,152,768]{2,1,0:T(8,128)(2,1)S(1)} all-to-all(bf16[8,152,768]{2,1,0:T(8,128)(2,1)S(1)} %bitcast.106), channel_id=1, replica_groups=mesh['exp'=8,'rep'=4] {'exp'}, dimensions={0} | all-to-all | bytes 3735552 | tf_op jit(solution)/shard_map/all_to_all | solution.py:207
  377.9 12.3 %fusion.144 = (bf16[3072]{0:T(1024)(128)(2,1)}, bf16[8,152,3072]{2,1,0:T(8,128)(2,1)}) fusion(f32[8,152,3072]{2,1,0:T(8,128)S(1)} %bitcast.94, f32[3072]{0:T(1024)S(1)} %bitcast.115, bf16[8,152,768]{2,1,0:T(8,128)(2,1)S(1)} %all_to_all.20, bf16[1,3072,768]{2,1,0:T(8,128)(2,1)S(1)} %bitcast.119), kind=kOutput, calls=%fused_computation.194 | convolution fusion | flops 5782631424 | bytes 29018112 | tf_op jit(solution)/shard_map/scd,fd->scf/dot_general | solution.py:222
  390.2 10.7 %fusion.55 = bf16[8,152,768]{2,1,0:T(8,128)(2,1)} fusion(bf16[8,152,3072]{2,1,0:T(8,128)(2,1)} %get-tuple-element.96, bf16[1,768,3072]{2,1,0:T(8,128)(2,1)} %param.25), kind=kOutput, calls=%fused_computation.87 | convolution fusion | flops 5738741760 | bytes 14057472 | tf_op jit(solution)/shard_map/scf,df->scd/dot_general | solution.py:236
  400.9 4.3 all-to-all-start.3
  405.5 10.7 %fusion.28 = bf16[1,3072,768]{2,1,0:T(8,128)(2,1)} fusion(bf16[8,152,3072]{2,1,0:T(8,128)(2,1)} %copy-done.10, bf16[8,152,768]{2,1,0:T(8,128)(2,1)} %copy-done.11), kind=kOutput, calls=%fused_computation.50 | convolution fusion | flops 5740167168 | bytes 14057472 | tf_op jit(solution)/shard_map/scf,scd->fd/dot_general | solution.py:218
  416.2 10.6 %fusion.27 = bf16[1,768,3072]{2,1,0:T(8,128)(2,1)} fusion(bf16[8,152,768]{2,1,0:T(8,128)(2,1)} %all-to-all-done, bf16[8,152,3072]{2,1,0:T(8,128)(2,1)} %get-tuple-element.96), kind=kOutput, calls=%fused_computation.49 | convolution fusion | flops 5740167168 | bytes 14057472 | tf_op jit(solution)/shard_map/scd,scf->df/dot_general | solution.py:226
  427.5 20.3 %all-to-all-done.3 = bf16[8,152,768]{2,1,0:T(8,128)(2,1)} async-done(((bf16[8,152,768]{2,1,0:T(8,128)(2,1)}), bf16[8,152,768]{2,1,0:T(8,128)(2,1)}, u32[]{:S(2)}, u32[]{:S(2)}) %all-to-all-start.3) | async-done | bytes 1867808 | tf_op jit(solution)/shard_map/all_to_all | solution.py:239
  447.7 3.6 fusion.85
  453.7 2.8 convert_add_fusion
  456.4 1.8 convolution_convert_fusion.2
  459.8 3.7 fusion.113
  464.1 12.5 %multiply_reduce_fusion = (f32[12,576]{1,0:T(8,128)S(1)}, f32[12,576,576]{1,2,0:T(8,128)}) fusion(f32[12,576,576]{1,2,0:T(8,128)} %get-tuple-element.84, f32[12,576]{1,0:T(8,128)S(1)} %copy-done.22, bf16[576,12,64]{0,2,1:T(8,128)(2,1)S(1)} %bitcast.97, bf16[576,12,64]{0,2,1:T(8,128)(2,1)} %bitcast.101), kind=kOutput, calls=%fused_computation.3 | convolution fusion | flops 521544960 | bytes 33675264 | tf_op jit(solution)/shard_map/while/body/eval_jaxpr/qhc,khc->hqk/dot_general | solution.py:80
  476.6 12.7 %multiply_convert_fusion = bf16[12,576,576]{1,2,0:T(8,128)(2,1)S(1)} fusion(f32[12,576,576]{1,2,0:T(8,128)} %get-tuple-element.93, f32[12,576,576]{1,2,0:T(8,128)} %get-tuple-element.84, f32[12,576]{1,0:T(8,128)S(1)} %get-tuple-element.92, f32[12,576]{1,0:T(8,128)S(1)} %copy-done.22), kind=kLoop, calls=%fused_computation.2 | loop fusion | flops 15925248 | bytes 39868416 | tf_op jit(solution)/shard_map/while/body/eval_jaxpr/convert_element_type | solution.py:86
  489.3 2.7 multiply_convert_fusion.1
  493.8 9.2 %fusion.82 = bf16[12,64,576]{2,1,0:T(8,128)(2,1)S(1)} fusion(bf16[576,12,64]{0,2,1:T(8,128)(2,1)S(1)} %bitcast.98, f32[12,576,576]{1,2,0:T(8,128)} %get-tuple-element.84, f32[12,576]{1,0:T(8,128)S(1)} %copy-done.22), kind=kOutput, calls=%fused_computation.122 | convolution fusion | flops 518012928 | bytes 17722368 | tf_op jit(solution)/shard_map/while/body/eval_jaxpr/hqk,qhc->khc/dot_general | solution.py:81
  504.0 6.3 fusion.88
  512.3 1.8 reduce_sum.267
  514.9 11.2 %all-reduce.11 = (bf16[1,3072]{1,0:T(2,128)(2,1)S(1)}, bf16[1,768]{1,0:T(2,128)(2,1)S(1)}) all-reduce(bf16[1,3072]{1,0:T(2,128)(2,1)S(1)} %broadcast_in_dim.62, bf16[1,768]{1,0:T(2,128)(2,1)S(1)} %broadcast_in_dim.66), channel_id=1, replica_groups=mesh['exp'=8,'rep'=4] {'rep'}, use_global_device_ids=true, to_apply=%region_36.37 | all-reduce | flops 3840 | bytes 15360 | tf_op jit(solution)/shard_map/psum | solution.py:232
  527.3 6.9 fusion.64
  534.3 39.1 %all-reduce.9 = (f32[768]{0:T(1024)S(1)}, f32[768]{0:T(1024)S(1)}, f32[768]{0:T(1024)S(1)}, f32[768]{0:T(1024)S(1)}, f32[768,8]{0,1:T(8,128)S(1)}) all-reduce(f32[768]{0:T(1024)S(1)} %get-tuple-element.50, f32[768]{0:T(1024)S(1)} %get-tuple-element.55, f32[768]{0:T(1024)S(1)} %copy-done.32, ...), channel_id=2, replica_groups=mesh['exp'=8,'rep'=4] {'exp','rep'}, use_global_device_ids=true, to_apply=%region_24.25.clone | all-reduce | flops 9216 | bytes 73728
  576.4 3.3 fusion.63
  579.7 19.2 %all-reduce.15.cloned.1.call-done = (bf16[1,768,3072]{2,1,0:T(8,128)(2,1)}, bf16[1,3072,768]{2,1,0:T(8,128)(2,1)}) async-done(((bf16[1,768,3072]{2,1,0:T(8,128)(2,1)}, bf16[1,3072,768]{2,1,0:T(8,128)(2,1)}), (bf16[1,768,3072]{2,1,0:T(8,128)(2,1)}, bf16[1,3072,768]{2,1,0:T(8,128)(2,1)})) %all-reduce.15.cloned.1.call-update) | async-done | bytes 9437200 | tf_op jit(solution)/shard_map/psum | solution.py:231
  598.8 7.5 broadcast_in_dim.61
  606.4 4.5 broadcast_in_dim.65
  610.8 93.4 %reduce-scatter.6.cloned.1.call-done = f32[24,768]{1,0:T(8,128)} async-done(((f32[768,768]{1,0:T(8,128)}), f32[24,768]{1,0:T(8,128)}) %reduce-scatter.6.cloned.1.call-update) | async-done | bytes 73744 | tf_op jit(solution)/shard_map/reduce_scatter | solution.py:296
  704.2 124.8 %reduce-scatter.4.cloned.1.call-done = f32[24,2304]{1,0:T(8,128)} async-done(((f32[768,2304]{1,0:T(8,128)}), f32[24,2304]{1,0:T(8,128)}) %reduce-scatter.4.cloned.1.call-update) | async-done | bytes 221200 | tf_op jit(solution)/shard_map/reduce_scatter | solution.py:295
  (178 shorter events, 34.5 us)
Async XLA Ops:
  7.2 66.5 %all-gather.4.cloned.1.call-start = ((), (), s32[]{:S(2)}) async-start(), calls=%async_computation.6 | async-start | bytes 3649536 | tf_op jit(solution)/shard_map/all_gather | solution.py:152
  7.9 121.5 %all-gather.6.cloned.1.call-start = ((), (), s32[]{:S(2)}) async-start(), calls=%async_computation.7 | async-start | bytes 1216512 | tf_op jit(solution)/shard_map/all_gather | solution.py:153
  57.7 20.7 %copy-start.41 = (f32[768]{0:T(1024)}, f32[768]{0:T(1024)S(1)}, u32[]{:S(2)}) copy-start(f32[768]{0:T(1024)S(1)} %convert_element_type.191) | copy-start | bytes 9220
  58.6 19.8 %copy-start.34 = (f32[768]{0:T(1024)}, f32[768]{0:T(1024)S(1)}, u32[]{:S(2)}) copy-start(f32[768]{0:T(1024)S(1)} %convert_element_type.190) | copy-start | bytes 9220
  58.6 392.7 %copy-start.24 = (f32[768]{0:T(1024)}, f32[768]{0:T(1024)S(1)}, u32[]{:S(2)}) copy-start(f32[768]{0:T(1024)S(1)} %convert_element_type.199) | copy-start | bytes 9220
  60.0 18.4 %copy-start.26 = (f32[576]{0:T(1024)}, f32[576]{0:T(1024)S(1)}, u32[]{:S(2)}) copy-start(f32[576]{0:T(1024)S(1)} %broadcast_multiply_fusion.5) | copy-start | bytes 6916
  61.6 16.8 %copy-start.37 = (f32[576]{0:T(1024)}, f32[576]{0:T(1024)S(1)}, u32[]{:S(2)}) copy-start(f32[576]{0:T(1024)S(1)} %add_rsqrt_fusion.1) | copy-start | bytes 6916
  80.1 11.2 %copy-start.1 = (bf16[576,768]{0,1:T(8,128)(2,1)}, bf16[576,768]{0,1:T(8,128)(2,1)S(1)}, u32[]{:S(2)}) copy-start(bf16[576,768]{0,1:T(8,128)(2,1)S(1)} %copy.62) | copy-start | bytes 2654212
  82.0 9.4 %copy-start.3 = (bf16[576,768]{0,1:T(8,128)(2,1)}, bf16[576,768]{0,1:T(8,128)(2,1)S(1)}, u32[]{:S(2)}) copy-start(bf16[576,768]{0,1:T(8,128)(2,1)S(1)} %copy.61) | copy-start | bytes 2654212
  91.4 8.6 %copy-start.13 = (bf16[576,768]{0,1:T(8,128)(2,1)S(1)}, bf16[576,768]{0,1:T(8,128)(2,1)}, u32[]{:S(2)}) copy-start(bf16[576,768]{0,1:T(8,128)(2,1)} %copy.60) | copy-start | bytes 2654212
  100.0 29.4 %copy-start.7 = (bf16[576,768]{1,0:T(8,128)(2,1)S(1)}, bf16[576,768]{1,0:T(8,128)(2,1)}, u32[]{:S(2)}) copy-start(bf16[576,768]{1,0:T(8,128)(2,1)} %param.17) | copy-start | bytes 2654212
  132.3 319.0 %copy-start.25 = (f32[576]{0:T(1024)}, f32[576]{0:T(1024)S(1)}, u32[]{:S(2)}) copy-start(f32[576]{0:T(1024)S(1)} %add_rsqrt_fusion) | copy-start | bytes 6916
  132.6 181.8 %copy-start.5 = (bf16[576,768]{1,0:T(8,128)(2,1)}, bf16[576,768]{1,0:T(8,128)(2,1)S(1)}, u32[]{:S(2)}) copy-start(bf16[576,768]{1,0:T(8,128)(2,1)S(1)} %add_convert_fusion.2) | copy-start | bytes 2654212
  136.2 5.1 copy-start.40
  136.2 5.2 copy-start.43
  136.2 49.0 %all-to-all-start = ((bf16[8,152,768]{2,1,0:T(8,128)(2,1)}), bf16[8,152,768]{2,1,0:T(8,128)(2,1)}, u32[]{:S(2)}, u32[]{:S(2)}) async-start(bf16[8,152,768]{2,1,0:T(8,128)(2,1)} %bitcast.105), calls=%async_computation | async-start | bytes 3735552 | tf_op jit(solution)/shard_map/all_to_all | solution.py:181
  197.9 34.2 %copy-start = (f32[8,152,3072]{2,1,0:T(8,128)}, f32[8,152,3072]{2,1,0:T(8,128)S(1)}, u32[]{:S(2)}) copy-start(f32[8,152,3072]{2,1,0:T(8,128)S(1)} %get-tuple-element.87) | copy-start | bytes 44826628
  244.5 4.5 copy-start.44
  244.5 70.3 %all-to-all-start.1 = ((bf16[8,152,768]{2,1,0:T(8,128)(2,1)}), bf16[8,152,768]{2,1,0:T(8,128)(2,1)}, u32[]{:S(2)}, u32[]{:S(2)}) async-start(bf16[8,152,768]{2,1,0:T(8,128)(2,1)} %add_convert_fusion), calls=%async_computation.1 | async-start | bytes 3735552 | tf_op jit(solution)/shard_map/all_to_all | solution.py:189
  314.9 3.1 copy-start.20
  318.0 5.0 copy-start.15
  318.0 59.8 %slice-start = ((s8[14942208]{0:T(1024)(128)(4,1)}), s8[4194304]{0:T(1024)(128)(4,1)S(1)}, s32[]{:S(2)}) async-start(s8[14942208]{0:T(1024)(128)(4,1)} %bitcast.93), calls=%async_computation.11 | async-start | bytes 8388608
  318.0 59.8 %slice-start.1 = ((s8[14942208]{0:T(1024)(128)(4,1)}), s8[4194304]{0:T(1024)(128)(4,1)S(1)}, s32[]{:S(2)}) async-start(s8[14942208]{0:T(1024)(128)(4,1)} %bitcast.93), calls=%async_computation.12 | async-start | bytes 8388608
  323.1 54.7 %slice-start.2 = ((s8[14942208]{0:T(1024)(128)(4,1)}), s8[4194304]{0:T(1024)(128)(4,1)S(1)}, s32[]{:S(2)}) async-start(s8[14942208]{0:T(1024)(128)(4,1)} %bitcast.93), calls=%async_computation.13 | async-start | bytes 8388608
  323.1 54.7 %slice-start.4 = ((s8[4718592]{0:T(1024)(128)(4,1)}), s8[4194304]{0:T(1024)(128)(4,1)S(1)}, s32[]{:S(2)}) async-start(s8[4718592]{0:T(1024)(128)(4,1)} %bitcast.118), calls=%async_computation.15 | async-start | bytes 8388608
  325.2 52.6 %slice-start.3 = ((s8[14942208]{0:T(1024)(128)(4,1)}), s8[2359296]{0:T(1024)(128)(4,1)S(1)}, s32[]{:S(2)}) async-start(s8[14942208]{0:T(1024)(128)(4,1)} %bitcast.93), calls=%async_computation.14 | async-start | bytes 4718592
  325.2 52.6 %slice-start.5 = ((s8[4718592]{0:T(1024)(128)(4,1)}), s8[524288]{0:T(1024)(128)(4,1)S(1)}, s32[]{:S(2)}) async-start(s8[4718592]{0:T(1024)(128)(4,1)} %bitcast.118), calls=%async_computation.16 | async-start | bytes 1048576
  377.8 12.3 %copy-start.11 = (bf16[8,152,768]{2,1,0:T(8,128)(2,1)}, bf16[8,152,768]{2,1,0:T(8,128)(2,1)S(1)}, u32[]{:S(2)}) copy-start(bf16[8,152,768]{2,1,0:T(8,128)(2,1)S(1)} %all_to_all.20) | copy-start | bytes 5603332
  400.9 46.9 %all-to-all-start.3 = ((bf16[8,152,768]{2,1,0:T(8,128)(2,1)}), bf16[8,152,768]{2,1,0:T(8,128)(2,1)}, u32[]{:S(2)}, u32[]{:S(2)}) async-start(bf16[8,152,768]{2,1,0:T(8,128)(2,1)} %fusion.55), calls=%async_computation.3 | async-start | bytes 3735552 | tf_op jit(solution)/shard_map/all_to_all | solution.py:239
  405.2 193.6 %all-reduce.15.cloned.1.call-start = ((), (), s32[]{:S(2)}) async-start(), calls=%async_computation.10 | async-start | bytes 18874368 | tf_op jit(solution)/shard_map/psum | solution.py:231
  426.8 277.5 %reduce-scatter.6.cloned.1.call-start = ((), (), s32[]{:S(2)}) async-start(), calls=%async_computation.9 | async-start | bytes 2433024 | tf_op jit(solution)/shard_map/reduce_scatter | solution.py:296
  459.8 4.2 copy-start.22
  463.6 365.4 %reduce-scatter.4.cloned.1.call-start = ((), (), s32[]{:S(2)}) async-start(), calls=%async_computation.8 | async-start | bytes 7299072 | tf_op jit(solution)/shard_map/reduce_scatter | solution.py:295
  476.6 12.7 %copy-start.4 = (bf16[576,768]{0,1:T(8,128)(2,1)S(1)}, bf16[576,768]{0,1:T(8,128)(2,1)}, u32[]{:S(2)}) copy-start(bf16[576,768]{0,1:T(8,128)(2,1)} %copy-done.3) | copy-start | bytes 2654212
  492.0 11.0 %copy-start.19 = (bf16[12,64,576]{2,1,0:T(8,128)(2,1)}, bf16[12,64,576]{2,1,0:T(8,128)(2,1)S(1)}, u32[]{:S(2)}) copy-start(bf16[12,64,576]{2,1,0:T(8,128)(2,1)S(1)} %multiply_convert_fusion.1) | copy-start | bytes 2654212
  493.7 9.3 %copy-start.14 = (bf16[12,64,576]{2,1,0:T(8,128)(2,1)}, bf16[12,64,576]{2,1,0:T(8,128)(2,1)S(1)}, u32[]{:S(2)}) copy-start(bf16[12,64,576]{2,1,0:T(8,128)(2,1)S(1)} %multiply_convert_fusion.2) | copy-start | bytes 2654212
  493.7 10.3 %copy-start.8 = (bf16[576,768]{1,0:T(8,128)(2,1)S(1)}, bf16[576,768]{1,0:T(8,128)(2,1)}, u32[]{:S(2)}) copy-start(bf16[576,768]{1,0:T(8,128)(2,1)} %param.17) | copy-start | bytes 2654212
  493.7 10.2 %copy-start.27 = (f32[576]{0:T(1024)S(1)}, f32[576]{0:T(1024)}, u32[]{:S(2)}) copy-start(f32[576]{0:T(1024)} %copy-done.26) | copy-start | bytes 6916
  493.8 10.2 %copy-start.35 = (f32[768]{0:T(1024)S(1)}, f32[768]{0:T(1024)}, u32[]{:S(2)}) copy-start(f32[768]{0:T(1024)} %copy-done.34) | copy-start | bytes 9220
  493.8 10.2 %copy-start.38 = (f32[576]{0:T(1024)S(1)}, f32[576]{0:T(1024)}, u32[]{:S(2)}) copy-start(f32[576]{0:T(1024)} %copy-done.37) | copy-start | bytes 6916
  493.8 10.2 %copy-start.42 = (f32[768]{0:T(1024)S(1)}, f32[768]{0:T(1024)}, u32[]{:S(2)}) copy-start(f32[768]{0:T(1024)} %copy-done.41) | copy-start | bytes 9220
  510.3 17.0 %copy-start.9 = (bf16[576,768]{1,0:T(8,128)(2,1)S(1)}, bf16[576,768]{1,0:T(8,128)(2,1)}, u32[]{:S(2)}) copy-start(bf16[576,768]{1,0:T(8,128)(2,1)} %param.17) | copy-start | bytes 2654212
  527.3 7.0 copy-start.23
  527.3 7.0 copy-start.32
  527.3 7.0 copy-start.33
  527.3 49.1 %copy-start.36 = (f32[768]{0:T(1024)S(1)}, f32[768]{0:T(1024)}, u32[]{:S(2)}) copy-start(f32[768]{0:T(1024)} %copy-done.34) | copy-start | bytes 9220
  527.3 49.1 %copy-start.39 = (f32[576]{0:T(1024)S(1)}, f32[576]{0:T(1024)}, u32[]{:S(2)}) copy-start(f32[576]{0:T(1024)} %copy-done.37) | copy-start | bytes 6916
  598.8 7.5 copy-start.12
  (12 other events, 25.7 us)
Sparse Core Ops, SparseCore 0:
  10.9 62.7 all-gather.3
  76.6 52.7 all-gather.5
  426.9 171.9 all-reduce.14
  604.6 99.6 reduce-scatter.5
  710.3 118.6 reduce-scatter.3
where the time goes:
time: 843 us; the launch traced here: 836 us
  waiting for transfers between devices  331 us (39%)
  blocking collectives  208 us (25%)
  matrix products  162 us (19%)
  other arithmetic  85.2 us (10%)
  local copies, waits for them, and re-layouts  20.4 us (2%)
  between operations  14.8 us (2%)
  starting transfers between devices  14.7 us (2%)
    reduce_scatter x1, waiting for transfers between devices, on_device(): lax.psum_scatter(grad_qkv_weight, ('exp', 'rep'), scatter_dimension=0, ti...  125 us
    reduce_scatter x1, waiting for transfers between devices, on_device(): lax.psum_scatter(grad_out_weight, ('exp', 'rep'), scatter_dimension=0, ti...  93.4 us
    unnamed x2, blocking collectives  81.3 us
    all_gather x1, blocking collectives, on_device(): lax.all_gather(w_router, ('exp', 'rep'), axis=0, tiled=True)  65.3 us
    all_to_all x1, blocking collectives, on_device(): lax.all_to_all(grad_slots.astype(jnp.bfloat16).reshape(experts, capacity,...  50.3 us
    all_to_all x1, waiting for transfers between devices, on_device(): lax.all_to_all(buffer, 'exp', split_axis=0, concat_axis=0, tiled=True)  43.8 us
    convert_element_type x1, other arithmetic, on_device(): active_part = jax.nn.gelu(pre_part, approximate=False).astype(jnp.bfloat16)  34.1 us
    all_to_all x1, waiting for transfers between devices, on_device(): lax.all_to_all(grad_received, 'exp', split_axis=0, concat_axis=0, tiled=T...  20.3 us
  transfers between devices with their start and end apart: 8, of which 7 were waited for; matrix products, arithmetic and copies ran while one was open for 19% of the time, Pallas kernels for 0%

commit v1 on v0

--- a/solution.py
+++ b/solution.py
@@ -228,7 +228,7 @@
     )
     grad_b_in = jnp.sum(grad_pre.astype(jnp.float32), axis=(0, 1))
     expert_sums = (
-        lax.psum(grad_w_in.astype(jnp.bfloat16), "rep").astype(jnp.float32),
+        jnp.sum(lax.all_gather(grad_w_in.astype(jnp.bfloat16), "rep"), axis=0).astype(jnp.float32),
         lax.psum(grad_b_in.astype(jnp.bfloat16), "rep").astype(jnp.float32),
         lax.psum(grad_w_back.astype(jnp.bfloat16), "rep").astype(jnp.float32),
         lax.psum(grad_b_back.astype(jnp.bfloat16), "rep").astype(jnp.float32),

time: 843 us -> 847 us (level)
  waiting for transfers between devices: 331 us -> 314 us
  other arithmetic: 85.2 us -> 101 us
    all_to_all x1, waiting for transfers between devices: 20.3 us -> 41.5 us  [on_device(): lax.all_to_all(grad_received, 'exp', split_axis=0, concat_axis=0, tiled=T...]
    psum x1, waiting for transfers between devices: 19.2 us -> 0.01 us  [on_device(): lax.psum(grad_w_back.astype(jnp.bfloat16), 'rep').astype(jnp.float32)]
    reduce_scatter x1, waiting for transfers between devices: 93.4 us -> 74.4 us  [on_device(): lax.psum_scatter(grad_out_weight, ('exp', 'rep'), scatter_dimension=0, ti...]
    reduce_sum x0 -> x1, other arithmetic: none -> 14 us  [on_device(): jnp.sum(lax.all_gather(grad_w_in.astype(jnp.bfloat16), 'rep'), axis=0)]
  transfers between devices with their start and end apart: 8 -> 9, of which waited for: 7 -> 6; matrix products, arithmetic and copies ran while one was open for 19% -> 23% of each run, Pallas kernels for 0% -> 0%
where the time goes in v1:
time: 847 us; the launch traced here: 840 us
  waiting for transfers between devices  314 us (37%)
  blocking collectives  209 us (25%)
  matrix products  161 us (19%)
  other arithmetic  101 us (12%)
  local copies, waits for them, and re-layouts  24 us (3%)
  between operations  15.1 us (2%)
  starting transfers between devices  14.8 us (2%)
    reduce_scatter x1, waiting for transfers between devices, on_device(): lax.psum_scatter(grad_qkv_weight, ('exp', 'rep'), scatter_dimension=0, ti...  125 us
    unnamed x2, blocking collectives  81.8 us
    reduce_scatter x1, waiting for transfers between devices, on_device(): lax.psum_scatter(grad_out_weight, ('exp', 'rep'), scatter_dimension=0, ti...  74.4 us
    all_gather x1, blocking collectives, on_device(): lax.all_gather(w_router, ('exp', 'rep'), axis=0, tiled=True)  65.3 us
    all_to_all x1, blocking collectives, on_device(): lax.all_to_all(grad_slots.astype(jnp.bfloat16).reshape(experts, capacity,...  50.3 us
    all_to_all x1, waiting for transfers between devices, on_device(): lax.all_to_all(buffer, 'exp', split_axis=0, concat_axis=0, tiled=True)  43.8 us
    all_to_all x1, waiting for transfers between devices, on_device(): lax.all_to_all(grad_received, 'exp', split_axis=0, concat_axis=0, tiled=T...  41.5 us
    convert_element_type x1, other arithmetic, on_device(): active_part = jax.nn.gelu(pre_part, approximate=False).astype(jnp.bfloat16)  34.1 us
  transfers between devices with their start and end apart: 9, of which 6 were waited for; matrix products, arithmetic and copies ran while one was open for 23% of the time, Pallas kernels for 0%

profile of v1, /device:TPU:0, one launch (start us, length us, event | category | flops | bytes accessed | tf_op | source)
XLA Modules:
  0.0 839.5 jit_solution(6037891693056788416)
XLA Ops:
  15.5 42.2 %all-reduce.10 = (bf16[768]{0:T(1024)(128)(2,1)S(1)}, bf16[768]{0:T(1024)(128)(2,1)S(1)}, bf16[768]{0:T(1024)(128)(2,1)S(1)}, bf16[768]{0:T(1024)(128)(2,1)S(1)}) all-reduce(bf16[768]{0:T(1024)(128)(2,1)S(1)} %dynamic-update-slice.1, bf16[768]{0:T(1024)(128)(2,1)S(1)} %dynamic-update-slice, ...), channel_id=1, replica_groups=mesh['exp'=8,'rep'=4] {'exp','rep'}, use_global_device_ids=true, to_apply=%add.1 | all-reduce | flops 3072 | bytes 12288
  64.7 9.0 %all-gather.6.cloned.1.call-done = bf16[768,2304]{1,0:T(8,128)(2,1)} async-done(((bf16[24,2304]{1,0:T(8,128)(2,1)}), bf16[768,2304]{1,0:T(8,128)(2,1)}) %all-gather.6.cloned.1.call-update) | async-done | bytes 3538960 | tf_op jit(solution)/shard_map/all_gather | solution.py:152
  73.7 4.7 convolution_convert_fusion
  80.1 1.9 copy.61
  83.3 8.0 fusion.140
  91.4 8.6 %fusion = f32[12,576]{1,0:T(8,128)S(1)} fusion(f32[12,576,576]{1,2,0:T(8,128)} %get-tuple-element.82, f32[12,576]{1,0:T(8,128)S(1)} %get-tuple-element.81), kind=kLoop, calls=%fused_computation.8 | loop fusion | flops 7955712 | bytes 15980544 | tf_op jit(solution)/shard_map/while/body/eval_jaxpr/reduce_sum | solution.py:70
  100.0 10.4 %fusion.80 = bf16[12,64,576]{2,1,0:T(8,128)(2,1)} fusion(bf16[576,12,64]{0,2,1:T(8,128)(2,1)S(1)} %bitcast.103, f32[12,576,576]{1,2,0:T(8,128)} %get-tuple-element.82, f32[12,576]{1,0:T(8,128)S(1)} %fusion, f32[12,576]{1,0:T(8,128)S(1)} %get-tuple-element.81), kind=kOutput, calls=%fused_computation.121 | convolution fusion | flops 521994240 | bytes 17750016 | tf_op jit(solution)/shard_map/while/body/eval_jaxpr/hqk,khc->qhc/dot_general | solution.py:72
  110.4 18.9 %all-gather.8.cloned.1.call-done = bf16[768,768]{1,0:T(8,128)(2,1)} async-done(((bf16[24,768]{1,0:T(8,128)(2,1)}), bf16[768,768]{1,0:T(8,128)(2,1)}) %all-gather.8.cloned.1.call-update) | async-done | bytes 1179664 | tf_op jit(solution)/shard_map/all_gather | solution.py:153
  129.4 2.6 fusion.141
  132.7 3.5 convolution_convert_fusion.1
  136.2 5.1 all-to-all-start
  141.4 43.8 %all-to-all-done = bf16[8,152,768]{2,1,0:T(8,128)(2,1)} async-done(((bf16[8,152,768]{2,1,0:T(8,128)(2,1)}), bf16[8,152,768]{2,1,0:T(8,128)(2,1)}, u32[]{:S(2)}, u32[]{:S(2)}) %all-to-all-start) | async-done | bytes 1867808 | tf_op jit(solution)/shard_map/all_to_all | solution.py:181
  185.2 12.7 %fusion.29 = (u8[152,3072]{1,0:T(8,128)(4,1)S(1)}, u8[152,3072]{1,0:T(8,128)(4,1)S(1)}, f32[8,152,3072]{2,1,0:T(8,128)S(1)}) fusion(f32[3072]{0:T(1024)S(1)} %bitcast.114, bf16[8,152,768]{2,1,0:T(8,128)(2,1)} %all-to-all-done, bf16[1,768,3072]{2,1,0:T(8,128)(2,1)} %param.25), kind=kOutput, calls=%fused_computation.54 | convolution fusion | flops 5789171712 | bytes 22474752 | tf_op jit(solution)/shard_map/scd,df->scf/dot_general | solution.py:182
  197.9 34.1 %fusion.3 = bf16[8,152,3072]{2,1,0:T(8,128)(2,1)S(1)} fusion(f32[8,152,3072]{2,1,0:T(8,128)S(1)} %get-tuple-element.85, f32[3072]{0:T(1024)S(1)} %bitcast.115, u8[152,3072]{1,0:T(8,128)(4,1)S(1)} %get-tuple-element.47, u8[152,3072]{1,0:T(8,128)(4,1)S(1)} %get-tuple-element.46), kind=kLoop, calls=%fused_computation.11 | loop fusion | flops 265224192 | bytes 23359488 | tf_op jit(solution)/shard_map/convert_element_type | solution.py:185
  232.1 3.1 copy-done.10
  235.1 9.4 %add_convert_fusion = bf16[8,152,768]{2,1,0:T(8,128)(2,1)} fusion(f32[768]{0:T(1024)S(1)} %convert_reduce_fusion.2, bf16[8,152,3072]{2,1,0:T(8,128)(2,1)S(1)} %fusion.3, bf16[1,3072,768]{2,1,0:T(8,128)(2,1)} %param.27), kind=kOutput, calls=%fused_computation.52 | convolution fusion | flops 5739675648 | bytes 14060544 | tf_op jit(solution)/shard_map/scf,fd->scd/dot_general | solution.py:186
  244.6 4.5 all-to-all-start.1
  249.1 65.3 %all-gather.1 = bf16[32,24,8]{1,2,0:T(8,128)(2,1)S(1)} all-gather(bf16[1,24,8]{1,2,0:T(8,128)(2,1)S(1)} %bitcast.117), channel_id=1, replica_groups=mesh['exp'=8,'rep'=4] {'exp','rep'}, dimensions={0}, use_global_device_ids=true | all-gather | bytes 12672 | tf_op jit(solution)/shard_map/all_gather | solution.py:156
  314.9 3.1 fusion.39
  318.1 5.0 fusion.67
  323.2 2.1 fusion.32
  325.3 2.3 fusion.30
  327.6 50.3 %all_to_all.20 = bf16[8,152,768]{2,1,0:T(8,128)(2,1)S(1)} all-to-all(bf16[8,152,768]{2,1,0:T(8,128)(2,1)S(1)} %bitcast.107), channel_id=1, replica_groups=mesh['exp'=8,'rep'=4] {'exp'}, dimensions={0} | all-to-all | bytes 3735552 | tf_op jit(solution)/shard_map/all_to_all | solution.py:207
  379.2 8.2 fusion.27
  387.7 15.0 %fusion.143 = (bf16[3072]{0:T(1024)(128)(2,1)}, bf16[8,152,3072]{2,1,0:T(8,128)(2,1)S(1)}) fusion(f32[8,152,3072]{2,1,0:T(8,128)} %copy-done, f32[3072]{0:T(1024)S(1)} %bitcast.116, bf16[8,152,768]{2,1,0:T(8,128)(2,1)} %copy-done.11, bf16[1,3072,768]{2,1,0:T(8,128)(2,1)} %param.27), kind=kOutput, calls=%fused_computation.194 | convolution fusion | flops 5782631424 | bytes 29018112 | tf_op jit(solution)/shard_map/scd,fd->scf/dot_general | solution.py:222
  402.6 3.1 copy-done.47
  405.7 9.4 %bitcast_convert_fusion.1 = bf16[768,3072]{1,0:T(8,128)(2,1)} fusion(bf16[8,152,768]{2,1,0:T(8,128)(2,1)} %all-to-all-done, bf16[8,152,3072]{2,1,0:T(8,128)(2,1)S(1)} %get-tuple-element.94), kind=kOutput, calls=%fused_computation.37 | convolution fusion | flops 5740167168 | bytes 14057472 | tf_op jit(solution)/shard_map/scd,scf->df/dot_general | solution.py:226
  415.1 10.8 %fusion.54 = bf16[8,152,768]{2,1,0:T(8,128)(2,1)} fusion(bf16[8,152,3072]{2,1,0:T(8,128)(2,1)} %copy-done.47, bf16[1,768,3072]{2,1,0:T(8,128)(2,1)} %param.25), kind=kOutput, calls=%fused_computation.87 | convolution fusion | flops 5738741760 | bytes 14057472 | tf_op jit(solution)/shard_map/scf,df->scd/dot_general | solution.py:236
  425.9 4.3 all-to-all-start.3
  430.9 41.5 %all-to-all-done.3 = bf16[8,152,768]{2,1,0:T(8,128)(2,1)} async-done(((bf16[8,152,768]{2,1,0:T(8,128)(2,1)}), bf16[8,152,768]{2,1,0:T(8,128)(2,1)}, u32[]{:S(2)}, u32[]{:S(2)}) %all-to-all-start.3) | async-done | bytes 1867808 | tf_op jit(solution)/shard_map/all_to_all | solution.py:239
  472.5 3.6 fusion.84
  478.3 2.8 convert_add_fusion
  484.4 3.7 fusion.112
  488.6 16.1 %multiply_reduce_fusion = (f32[12,576]{1,0:T(8,128)S(1)}, f32[12,576,576]{1,2,0:T(8,128)}) fusion(f32[12,576,576]{1,2,0:T(8,128)} %get-tuple-element.82, f32[12,576]{1,0:T(8,128)S(1)} %copy-done.24, bf16[576,12,64]{0,2,1:T(8,128)(2,1)S(1)} %bitcast.96, bf16[576,12,64]{0,2,1:T(8,128)(2,1)} %bitcast.102), kind=kOutput, calls=%fused_computation.3 | convolution fusion | flops 521544960 | bytes 33675264 | tf_op jit(solution)/shard_map/while/body/eval_jaxpr/qhc,khc->hqk/dot_general | solution.py:80
  504.8 12.5 %multiply_convert_fusion = bf16[12,576,576]{1,2,0:T(8,128)(2,1)S(1)} fusion(f32[12,576,576]{1,2,0:T(8,128)} %get-tuple-element.91, f32[12,576,576]{1,2,0:T(8,128)} %get-tuple-element.82, f32[12,576]{1,0:T(8,128)S(1)} %get-tuple-element.90, f32[12,576]{1,0:T(8,128)S(1)} %copy-done.24), kind=kLoop, calls=%fused_computation.2 | loop fusion | flops 15925248 | bytes 39868416 | tf_op jit(solution)/shard_map/while/body/eval_jaxpr/convert_element_type | solution.py:86
  517.3 2.7 multiply_convert_fusion.1
  521.7 9.3 %fusion.81 = bf16[12,64,576]{2,1,0:T(8,128)(2,1)S(1)} fusion(bf16[576,12,64]{0,2,1:T(8,128)(2,1)S(1)} %bitcast.97, f32[12,576,576]{1,2,0:T(8,128)} %get-tuple-element.82, f32[12,576]{1,0:T(8,128)S(1)} %copy-done.24), kind=kOutput, calls=%fused_computation.122 | convolution fusion | flops 518012928 | bytes 17722368 | tf_op jit(solution)/shard_map/while/body/eval_jaxpr/hqk,qhc->khc/dot_general | solution.py:81
  532.0 6.2 fusion.87
  539.7 1.9 reduce_sum.280
  541.6 12.0 %all-reduce.11 = (bf16[1,3072]{1,0:T(2,128)(2,1)S(1)}, bf16[1,768]{1,0:T(2,128)(2,1)S(1)}) all-reduce(bf16[1,3072]{1,0:T(2,128)(2,1)S(1)} %broadcast_in_dim.55, bf16[1,768]{1,0:T(2,128)(2,1)S(1)} %broadcast_in_dim.59), channel_id=1, replica_groups=mesh['exp'=8,'rep'=4] {'rep'}, use_global_device_ids=true, to_apply=%region_36.37 | all-reduce | flops 3840 | bytes 15360 | tf_op jit(solution)/shard_map/psum | solution.py:232
  554.8 7.0 broadcast_in_dim.58
  561.8 4.1 fusion.63
  565.9 39.6 %all-reduce.9 = (f32[768]{0:T(1024)S(1)}, f32[768]{0:T(1024)S(1)}, f32[768]{0:T(1024)S(1)}, f32[768]{0:T(1024)S(1)}, f32[768,8]{0,1:T(8,128)S(1)}) all-reduce(f32[768]{0:T(1024)S(1)} %get-tuple-element.50, f32[768]{0:T(1024)S(1)} %get-tuple-element.55, f32[768]{0:T(1024)S(1)} %copy-done.33, ...), channel_id=3, replica_groups=mesh['exp'=8,'rep'=4] {'exp','rep'}, use_global_device_ids=true, to_apply=%region_24.25.clone | all-reduce | flops 9216 | bytes 73728
  608.6 3.3 fusion.62
  611.9 14.0 %reduce_sum.278 = bf16[768,3072]{1,0:T(8,128)(2,1)} reduce(bf16[4,768,3072]{2,1,0:T(8,128)(2,1)} %bitcast.93, bf16[]{:T(256)} %constant.50.clone.1), dimensions={0}, to_apply=%region_34.35 | reduce | flops 7077888 | bytes 23592962 | tf_op jit(solution)/shard_map/reduce_sum | solution.py:231
  625.9 7.4 bitcast_convert_fusion.2
  633.3 74.4 %reduce-scatter.6.cloned.1.call-done = f32[24,768]{1,0:T(8,128)} async-done(((f32[768,768]{1,0:T(8,128)}), f32[24,768]{1,0:T(8,128)}) %reduce-scatter.6.cloned.1.call-update) | async-done | bytes 73744 | tf_op jit(solution)/shard_map/reduce_scatter | solution.py:296
  707.7 124.7 %reduce-scatter.4.cloned.1.call-done = f32[24,2304]{1,0:T(8,128)} async-done(((f32[768,2304]{1,0:T(8,128)}), f32[24,2304]{1,0:T(8,128)}) %reduce-scatter.4.cloned.1.call-update) | async-done | bytes 221200 | tf_op jit(solution)/shard_map/reduce_scatter | solution.py:295
  (177 shorter events, 36.1 us)
Async XLA Ops:
  7.2 66.5 %all-gather.6.cloned.1.call-start = ((), (), s32[]{:S(2)}) async-start(), calls=%async_computation.6 | async-start | bytes 3649536 | tf_op jit(solution)/shard_map/all_gather | solution.py:152
  7.9 121.5 %all-gather.8.cloned.1.call-start = ((), (), s32[]{:S(2)}) async-start(), calls=%async_computation.7 | async-start | bytes 1216512 | tf_op jit(solution)/shard_map/all_gather | solution.py:153
  57.7 20.7 %copy-start.41 = (f32[768]{0:T(1024)}, f32[768]{0:T(1024)S(1)}, u32[]{:S(2)}) copy-start(f32[768]{0:T(1024)S(1)} %convert_element_type.205) | copy-start | bytes 9220
  58.6 19.8 %copy-start.35 = (f32[768]{0:T(1024)}, f32[768]{0:T(1024)S(1)}, u32[]{:S(2)}) copy-start(f32[768]{0:T(1024)S(1)} %convert_element_type.204) | copy-start | bytes 9220
  58.6 417.4 %copy-start.25 = (f32[768]{0:T(1024)}, f32[768]{0:T(1024)S(1)}, u32[]{:S(2)}) copy-start(f32[768]{0:T(1024)S(1)} %convert_element_type.213) | copy-start | bytes 9220
  60.0 18.4 %copy-start.27 = (f32[576]{0:T(1024)}, f32[576]{0:T(1024)S(1)}, u32[]{:S(2)}) copy-start(f32[576]{0:T(1024)S(1)} %broadcast_multiply_fusion.5) | copy-start | bytes 6916
  61.6 16.8 %copy-start.37 = (f32[576]{0:T(1024)}, f32[576]{0:T(1024)S(1)}, u32[]{:S(2)}) copy-start(f32[576]{0:T(1024)S(1)} %add_rsqrt_fusion.1) | copy-start | bytes 6916
  80.1 11.3 %copy-start.1 = (bf16[576,768]{0,1:T(8,128)(2,1)}, bf16[576,768]{0,1:T(8,128)(2,1)S(1)}, u32[]{:S(2)}) copy-start(bf16[576,768]{0,1:T(8,128)(2,1)S(1)} %copy.62) | copy-start | bytes 2654212
  82.0 9.4 %copy-start.3 = (bf16[576,768]{0,1:T(8,128)(2,1)}, bf16[576,768]{0,1:T(8,128)(2,1)S(1)}, u32[]{:S(2)}) copy-start(bf16[576,768]{0,1:T(8,128)(2,1)S(1)} %copy.61) | copy-start | bytes 2654212
  91.4 8.6 %copy-start.12 = (bf16[576,768]{0,1:T(8,128)(2,1)S(1)}, bf16[576,768]{0,1:T(8,128)(2,1)}, u32[]{:S(2)}) copy-start(bf16[576,768]{0,1:T(8,128)(2,1)} %copy.60) | copy-start | bytes 2654212
  100.0 29.4 %copy-start.7 = (bf16[576,768]{1,0:T(8,128)(2,1)S(1)}, bf16[576,768]{1,0:T(8,128)(2,1)}, u32[]{:S(2)}) copy-start(bf16[576,768]{1,0:T(8,128)(2,1)} %param.17) | copy-start | bytes 2654212
  132.3 343.7 %copy-start.26 = (f32[576]{0:T(1024)}, f32[576]{0:T(1024)S(1)}, u32[]{:S(2)}) copy-start(f32[576]{0:T(1024)S(1)} %add_rsqrt_fusion) | copy-start | bytes 6916
  132.7 181.9 %copy-start.5 = (bf16[576,768]{1,0:T(8,128)(2,1)}, bf16[576,768]{1,0:T(8,128)(2,1)S(1)}, u32[]{:S(2)}) copy-start(bf16[576,768]{1,0:T(8,128)(2,1)S(1)} %add_convert_fusion.2) | copy-start | bytes 2654212
  136.2 5.1 copy-start.39
  136.2 5.2 copy-start.43
  136.2 49.0 %all-to-all-start = ((bf16[8,152,768]{2,1,0:T(8,128)(2,1)}), bf16[8,152,768]{2,1,0:T(8,128)(2,1)}, u32[]{:S(2)}, u32[]{:S(2)}) async-start(bf16[8,152,768]{2,1,0:T(8,128)(2,1)} %bitcast.106), calls=%async_computation | async-start | bytes 3735552 | tf_op jit(solution)/shard_map/all_to_all | solution.py:181
  197.9 34.2 %copy-start = (f32[8,152,3072]{2,1,0:T(8,128)}, f32[8,152,3072]{2,1,0:T(8,128)S(1)}, u32[]{:S(2)}) copy-start(f32[8,152,3072]{2,1,0:T(8,128)S(1)} %get-tuple-element.85) | copy-start | bytes 44826628
  232.0 3.1 copy-start.10
  244.6 4.5 copy-start.44
  244.6 70.4 %all-to-all-start.1 = ((bf16[8,152,768]{2,1,0:T(8,128)(2,1)}), bf16[8,152,768]{2,1,0:T(8,128)(2,1)}, u32[]{:S(2)}, u32[]{:S(2)}) async-start(bf16[8,152,768]{2,1,0:T(8,128)(2,1)} %add_convert_fusion), calls=%async_computation.1 | async-start | bytes 3735552 | tf_op jit(solution)/shard_map/all_to_all | solution.py:189
  249.0 305.8 %all-reduce.14.cloned.1.call-start = ((), (), s32[]{:S(2)}) async-start(), calls=%async_computation.10 | async-start | bytes 9437184 | tf_op jit(solution)/shard_map/psum | solution.py:233
  314.9 3.1 copy-start.22
  318.1 5.0 copy-start.15
  323.1 56.0 %slice-start = ((s8[7471104]{0:T(1024)(128)(4,1)}), s8[4194304]{0:T(1024)(128)(4,1)S(1)}, s32[]{:S(2)}) async-start(s8[7471104]{0:T(1024)(128)(4,1)} %bitcast.100), calls=%async_computation.12 | async-start | bytes 8388608
  325.3 53.8 %slice-start.1 = ((s8[7471104]{0:T(1024)(128)(4,1)}), s8[3276800]{0:T(1024)(128)(4,1)S(1)}, s32[]{:S(2)}) async-start(s8[7471104]{0:T(1024)(128)(4,1)} %bitcast.100), calls=%async_computation.13 | async-start | bytes 6553600
  387.4 224.5 %all-gather.10.cloned.1.call-start = ((), (), s32[]{:S(2)}) async-start(), calls=%async_computation.11 | async-start | bytes 23592960 | tf_op jit(solution)/shard_map/all_gather | solution.py:231
  402.6 3.1 copy-start.47
  425.9 46.6 %all-to-all-start.3 = ((bf16[8,152,768]{2,1,0:T(8,128)(2,1)}), bf16[8,152,768]{2,1,0:T(8,128)(2,1)}, u32[]{:S(2)}, u32[]{:S(2)}) async-start(bf16[8,152,768]{2,1,0:T(8,128)(2,1)} %fusion.54), calls=%async_computation.3 | async-start | bytes 3735552 | tf_op jit(solution)/shard_map/all_to_all | solution.py:239
  430.2 277.5 %reduce-scatter.6.cloned.1.call-start = ((), (), s32[]{:S(2)}) async-start(), calls=%async_computation.9 | async-start | bytes 2433024 | tf_op jit(solution)/shard_map/reduce_scatter | solution.py:296
  478.3 2.8 copy-start.46
  484.4 4.2 copy-start.24
  488.2 344.3 %reduce-scatter.4.cloned.1.call-start = ((), (), s32[]{:S(2)}) async-start(), calls=%async_computation.8 | async-start | bytes 7299072 | tf_op jit(solution)/shard_map/reduce_scatter | solution.py:295
  504.8 12.5 %copy-start.4 = (bf16[576,768]{0,1:T(8,128)(2,1)S(1)}, bf16[576,768]{0,1:T(8,128)(2,1)}, u32[]{:S(2)}) copy-start(bf16[576,768]{0,1:T(8,128)(2,1)} %copy-done.3) | copy-start | bytes 2654212
  520.0 11.1 %copy-start.20 = (bf16[12,64,576]{2,1,0:T(8,128)(2,1)}, bf16[12,64,576]{2,1,0:T(8,128)(2,1)S(1)}, u32[]{:S(2)}) copy-start(bf16[12,64,576]{2,1,0:T(8,128)(2,1)S(1)} %multiply_convert_fusion.1) | copy-start | bytes 2654212
  521.7 9.4 %copy-start.13 = (bf16[12,64,576]{2,1,0:T(8,128)(2,1)}, bf16[12,64,576]{2,1,0:T(8,128)(2,1)S(1)}, u32[]{:S(2)}) copy-start(bf16[12,64,576]{2,1,0:T(8,128)(2,1)S(1)} %multiply_convert_fusion.2) | copy-start | bytes 2654212
  521.7 10.3 %copy-start.8 = (bf16[576,768]{1,0:T(8,128)(2,1)S(1)}, bf16[576,768]{1,0:T(8,128)(2,1)}, u32[]{:S(2)}) copy-start(bf16[576,768]{1,0:T(8,128)(2,1)} %param.17) | copy-start | bytes 2654212
  521.7 10.3 %copy-start.28 = (f32[576]{0:T(1024)S(1)}, f32[576]{0:T(1024)}, u32[]{:S(2)}) copy-start(f32[576]{0:T(1024)} %copy-done.27) | copy-start | bytes 6916
  521.7 10.3 %copy-start.36 = (f32[768]{0:T(1024)S(1)}, f32[768]{0:T(1024)}, u32[]{:S(2)}) copy-start(f32[768]{0:T(1024)} %copy-done.35) | copy-start | bytes 9220
  521.7 10.3 %copy-start.38 = (f32[576]{0:T(1024)S(1)}, f32[576]{0:T(1024)}, u32[]{:S(2)}) copy-start(f32[576]{0:T(1024)} %copy-done.37) | copy-start | bytes 6916
  521.7 10.3 %copy-start.42 = (f32[768]{0:T(1024)S(1)}, f32[768]{0:T(1024)}, u32[]{:S(2)}) copy-start(f32[768]{0:T(1024)} %copy-done.41) | copy-start | bytes 9220
  538.3 3.3 copy-start.40
  554.8 7.0 copy-start.9
  554.8 7.0 copy-start.14
  554.8 7.0 copy-start.19
  554.8 7.0 copy-start.21
  554.8 7.0 copy-start.45
  561.8 4.1 copy-start.33
  561.8 4.1 copy-start.34
  (11 other events, 20.7 us)
Sparse Core Ops, SparseCore 0:
  10.9 62.7 all-gather.5
  76.6 52.7 all-gather.7
  387.5 91.5 all-reduce.13
  481.1 121.1 all-gather.9
  608.0 99.6 reduce-scatter.5
  713.8 118.5 reduce-scatter.3
